TPU v7x, 128 devices: a whole 4x4x4 slice. The times are simulated.
128 devices in a mesh: row: 8 (over y, core), col: 16 (over z, x).
Axes of the slice: x: 4, y: 4, z: 4, core: 2. Of those that a mesh axis runs over, the one named last changes fastest.
Arguments:
- kernel_panel: float32 [64, 32768], P(None, ('row', 'col')), may hold values from -4 to 16, as said below
- kernel_slab: float32 [32768, 4096], P('row', 'col'), may hold values from -4 to 20, as said below
- targets: float32 [256, 32768], P(None, ('row', 'col')), may hold values from -6 to 6
Outputs:
- updated_slab: float32 [32768, 4096], P('row', 'col')
- solved_targets: float32 [256, 32768], P('col', 'row')
- panel_factor: float32 [64, 32768], P(None, ('row', 'col'))
Inputs may be any that keep to these rules, and one draw needn't show every extreme that they name: kernel_panel[:, 0:64] is symmetric and positive definite. `kernel_slab`: rows 0 to 63 equal kernel_panel[:, 32768 - 4096 : 32768]; the last 4096 rows form a symmetric matrix.
All inputs are finite; a program needn't handle non-finite values.
Results may differ from a plain program's by a relative error of at most 0.00018.
Values sent between devices are 32-bit elements; how exact they have to be, the bound alone decides.
No kernel may reach another device: no remote copies, remote signals or barrier semaphores. Data moves between devices by JAX's collectives and lax.ppermute only.
A program may use at most 64 MiB of HBM per device.

v0:
```python
import jax
import jax.numpy as jnp
from jax import lax
from jax.sharding import PartitionSpec as P


def spread(block, axis, source):
    block = jnp.where(lax.axis_index(axis) == source, block, jnp.zeros_like(block))
    return lax.psum(block, axis)


def lower_solve(factor, values):
    return jax.scipy.linalg.solve_triangular(factor, values, lower=True)


def body(kernel_panel, kernel_slab, targets):
    highest = lax.Precision.HIGHEST
    panel_width = kernel_panel.shape[0]
    row_count = lax.axis_size("row")
    row_index = lax.axis_index("row")
    flat_index = lax.axis_index(("row", "col"))
    corner_rows = jnp.concatenate([kernel_panel[:, :panel_width], targets[:, :panel_width]], 0)
    shared = spread(corner_rows, ("row", "col"), 0)
    lower_factor = jnp.linalg.cholesky(shared[:panel_width])
    panel_factor = lower_solve(lower_factor, kernel_panel)
    gathered = lax.all_gather(panel_factor, "col", axis=1, tiled=True)
    slab_factor = spread(panel_factor, "row", row_count - 1)
    product = lax.dot_general(
        gathered,
        slab_factor,
        (((0,), (0,)), ((), ())),
        precision=highest,
        preferred_element_type=jnp.float32,
    )
    update = kernel_slab - product
    head_rows = jnp.where(row_index == 0, slab_factor, update[:panel_width])
    updated_slab = jnp.concatenate([head_rows, update[panel_width:]], 0)
    solved_lead = lower_solve(lower_factor, shared[panel_width:].T).T
    result = targets - jnp.dot(
        solved_lead, panel_factor, precision=highest, preferred_element_type=jnp.float32
    )
    head_cols = jnp.where(flat_index == 0, solved_lead, result[:, :panel_width])
    result = jnp.concatenate([head_cols, result[:, panel_width:]], 1)
    solved_targets = lax.all_to_all(result, "col", split_axis=0, concat_axis=1, tiled=True)
    return (updated_slab, solved_targets, panel_factor)


def solution(mesh):
    in_specs = (P(None, ("row", "col")), P("row", "col"), P(None, ("row", "col")))
    out_specs = (P("row", "col"), P("col", "row"), P(None, ("row", "col")))
    return jax.shard_map(body, mesh=mesh, in_specs=in_specs, out_specs=out_specs, check_vma=False)
```

profile of v0, /device:TPU:0, one launch (start us, length us, event | category | flops | bytes accessed | tf_op | source)
XLA Modules:
  0.0 286.8 jit_solution(15664791899250229156)
XLA Ops:
  7.2 0.0 all-reduce.3.cloned.1.call-start
  7.2 0.8 slice.34
  8.0 0.1 copy.22
  8.1 1.1 copy.17
  9.2 0.7 maximum_select_fusion
  9.9 0.0 all-reduce.3.cloned.1.call-update
  9.9 0.0 all-reduce.5.cloned.1.call-start
  10.0 143.3 %all-reduce.3.cloned.1.call-done = f32[320,64]{0,1:T(8,128)} async-done(((f32[320,64]{0,1:T(8,128)}), f32[320,64]{0,1:T(8,128)}) %all-reduce.3.cloned.1.call-update) | async-done | bytes 81936 | tf_op jit(solution)/shard_map/psum | solution.py:9
  153.3 0.8 slice.43
  154.1 0.1 copy.18
  154.1 0.8 fusion.5
  154.9 5.8 %cholesky.18 = f32[64,64]{1,0:T(8,128)S(1)} custom-call(f32[64,64]{1,0:T(8,128)S(1)} %fusion.5), custom_call_target="Cholesky" | custom-call | tf_op jit(solution)/shard_map/jit(cholesky)/cholesky | solution.py:24
  160.8 0.6 compare_reduce_fusion
  161.4 0.7 fusion.1
  162.1 4.9 %custom-call.7 = f32[1,64,64]{1,2,0:T(8,128)S(1)} custom-call(f32[1,64,64]{2,1,0:T(8,128)S(1)} %fusion.1), custom_call_target="InvertDiagBlocksLowerTriangular" | custom-call | tf_op jit(solution)/shard_map/jit(_solve_triangular)/triangular_solve | solution.py:13
  167.0 1.8 broadcast_select_fusion
  168.8 0.0 all-reduce.5.cloned.1.call-update
  168.8 0.0 all-gather.2.cloned.1.call-start
  168.8 0.7 all-gather.2.cloned.1.call-update
  169.5 1.2 fusion
  170.7 1.3 convolution_subtract_fusion.1
  172.0 0.8 copy.20
  172.9 5.6 %all-to-all-start = ((f32[16,16,256]{2,1,0:T(8,128)}), f32[16,16,256]{2,1,0:T(8,128)S(1)}, u32[]{:S(2)}, u32[]{:S(2)}) async-start(f32[16,16,256]{2,1,0:T(8,128)} %bitcast.7), calls=%async_computation | async-start | bytes 524288 | tf_op jit(solution)/shard_map/all_to_all | solution.py:44
  178.5 8.7 %all-to-all-done = f32[16,16,256]{2,1,0:T(8,128)S(1)} async-done(((f32[16,16,256]{2,1,0:T(8,128)}), f32[16,16,256]{2,1,0:T(8,128)S(1)}, u32[]{:S(2)}, u32[]{:S(2)}) %all-to-all-start) | async-done | bytes 262176 | tf_op jit(solution)/shard_map/all_to_all | solution.py:44
  187.2 0.7 copy.23
  187.9 38.0 %all-reduce.5.cloned.1.call-done = f32[64,256]{1,0:T(8,128)} async-done(((f32[64,256]{1,0:T(8,128)}), f32[64,256]{1,0:T(8,128)}) %all-reduce.5.cloned.1.call-update) | async-done | bytes 65552 | tf_op jit(solution)/shard_map/psum | solution.py:9
  225.9 45.2 %all-gather.2.cloned.1.call-done = f32[64,4096]{1,0:T(8,128)} async-done(((f32[64,256]{1,0:T(8,128)}), f32[64,4096]{1,0:T(8,128)}) %all-gather.2.cloned.1.call-update) | async-done | bytes 1048592 | tf_op jit(solution)/shard_map/all_gather | solution.py:26
  271.1 6.0 %convolution_subtract_fusion = f32[4096,256]{1,0:T(8,128)S(1)} fusion(f32[4096,256]{1,0:T(8,128)} %param.6, f32[64,4096]{1,0:T(8,128)} %all-gather.2.cloned.1.call-done, f32[64,256]{1,0:T(8,128)} %all-reduce.5.cloned.1.call-done), kind=kOutput, calls=%fused_computation | convolution fusion | flops 806354944 | bytes 9502720 | tf_op jit(solution)/shard_map/dot_general | solution.py:28
  277.1 0.0 copy-start
  277.1 0.3 slice.45
  277.4 0.6 copy-done
  278.0 2.3 pad_maximum_fusion
  (6 shorter events, 0.1 us)
Async XLA Ops:
  7.2 146.1 %all-reduce.3.cloned.1.call-start = ((), (), s32[]{:S(2)}) async-start(), calls=%async_computation.1 | async-start | bytes 196608 | tf_op jit(solution)/shard_map/psum | solution.py:9
  9.9 216.0 %all-reduce.5.cloned.1.call-start = ((), (), s32[]{:S(2)}) async-start(), calls=%async_computation.2 | async-start | bytes 131072 | tf_op jit(solution)/shard_map/psum | solution.py:9
  168.8 102.3 %all-gather.2.cloned.1.call-start = ((), (), s32[]{:S(2)}) async-start(), calls=%async_computation.3 | async-start | bytes 1114112 | tf_op jit(solution)/shard_map/all_gather | solution.py:26
  172.9 14.3 %all-to-all-start = ((f32[16,16,256]{2,1,0:T(8,128)}), f32[16,16,256]{2,1,0:T(8,128)S(1)}, u32[]{:S(2)}, u32[]{:S(2)}) async-start(f32[16,16,256]{2,1,0:T(8,128)} %bitcast.7), calls=%async_computation | async-start | bytes 524288 | tf_op jit(solution)/shard_map/all_to_all | solution.py:44
  277.1 0.8 copy-start
Sparse Core Ops, SparseCore 0:
  13.3 139.9 all-reduce.2
  168.9 56.9 all-reduce.4
  228.6 42.4 all-gather.1
where the time goes:
time: 287 us
  waiting for transfers between devices  236 us (82%)
  other arithmetic  15.9 us (6%)
  between operations  13.9 us (5%)
  matrix products  10.2 us (4%)
  starting transfers between devices  5.75 us (2%)
  local copies, waits for them, and re-layouts  5.16 us (2%)
    psum x2, waiting for transfers between devices, spread(): return lax.psum(block, axis)  181 us
    all_gather x1, waiting for transfers between devices, body(): gathered = lax.all_gather(panel_factor, 'col', axis=1, tiled=True)  45.2 us
    all_to_all x1, waiting for transfers between devices, body(): lax.all_to_all(result, 'col', split_axis=0, concat_axis=1, tiled=True)  8.69 us
    another operation x3, other arithmetic, body(): lower_factor = jnp.linalg.cholesky(shared[:panel_width])  6.52 us
    dot_general x1, matrix products, body(): lax.dot_general(gathered, slab_factor, (((0,), (0,)), ((), ())), precisio...  6 us
  transfers between devices with their start and end apart: 4, of which 4 were waited for; matrix products, arithmetic and copies ran while one was open for 1% of the time, Pallas kernels for 0%

commit v1 on v0

--- a/solution.py
+++ b/solution.py
@@ -2,6 +2,35 @@
 import jax.numpy as jnp
 from jax import lax
 from jax.sharding import PartitionSpec as P
+
+
+def process_quarters_over_axis(frame, in_dim, array_in):
+    item_now, t_next = (frame.shape[:in_dim], frame.shape[in_dim + 1 :])
+    z_new = jnp.moveaxis(frame.reshape(*item_now, array_in, -1, *t_next), in_dim, 0)
+    return z_new
+
+
+def pair_strings(local_x, out_dim):
+    local_x = jnp.moveaxis(local_x, 0, out_dim)
+    f_now = local_x.shape
+    ready = local_x.reshape(
+        *f_now[:out_dim], f_now[out_dim] * f_now[out_dim + 1], *f_now[out_dim + 2 :]
+    )
+    return ready
+
+
+def _choose_record(x_local, inputs, axis_key, patch):
+    met_up, tile_out = (lax.axis_size(axis_key), lax.axis_index(axis_key))
+    block_out = process_quarters_over_axis(patch, x_local, met_up)
+    k0 = 1
+    copies = [block_out[tile_out]]
+    while k0 < met_up:
+        f_next = block_out[tile_out ^ k0]
+        copies.append(lax.ppermute(f_next, axis_key, [(s, s ^ k0) for s in range(met_up)]))
+        k0 += 1
+    block_out = jnp.stack(copies)[tile_out ^ jnp.arange(met_up)]
+    moved = pair_strings(block_out, inputs)
+    return moved
 
 
 def spread(block, axis, source):
@@ -41,7 +70,7 @@
     )
     head_cols = jnp.where(flat_index == 0, solved_lead, result[:, :panel_width])
     result = jnp.concatenate([head_cols, result[:, panel_width:]], 1)
-    solved_targets = lax.all_to_all(result, "col", split_axis=0, concat_axis=1, tiled=True)
+    solved_targets = _choose_record(0, 1, "col", result)
     return (updated_slab, solved_targets, panel_factor)
 
 

time: 287 us -> 289 us (level)
  starting transfers between devices: 5.75 us -> 20.7 us
  waiting for transfers between devices: 236 us -> 223 us
    ppermute x0 -> x15, waiting for transfers between devices: none -> 47.8 us  [_choose_record(): lax.ppermute(f_next, axis_key, [(s, s ^ k0) for s in range(met_up)])]
    psum x2, waiting for transfers between devices: 181 us -> 143 us  [spread(): return lax.psum(block, axis)]
    ppermute x0 -> x15, starting transfers between devices: none -> 20.6 us  [_choose_record(): lax.ppermute(f_next, axis_key, [(s, s ^ k0) for s in range(met_up)])]
    all_gather x1, waiting for transfers between devices: 45.2 us -> 32.4 us  [body(): gathered = lax.all_gather(panel_factor, 'col', axis=1, tiled=True)]
    all_to_all x1 -> x0, waiting for transfers between devices: 8.69 us -> none  [body(): lax.all_to_all(result, 'col', split_axis=0, concat_axis=1, tiled=True)]
    all_to_all x1 -> x0, starting transfers between devices: 5.63 us -> none  [body(): lax.all_to_all(result, 'col', split_axis=0, concat_axis=1, tiled=True)]
  transfers between devices with their start and end apart: 4 -> 18, of which waited for: 4 -> 12; matrix products, arithmetic and copies ran while one was open for 1% -> 0% of each run, Pallas kernels for 0% -> 0%
where the time goes in v1:
time: 289 us
  waiting for transfers between devices  223 us (77%)
  starting transfers between devices  20.7 us (7%)
  other arithmetic  15.9 us (6%)
  between operations  14.1 us (5%)
  matrix products  9.37 us (3%)
  local copies, waits for them, and re-layouts  5.15 us (2%)
    psum x2, waiting for transfers between devices, spread(): return lax.psum(block, axis)  143 us
    ppermute x15, waiting for transfers between devices, _choose_record(): lax.ppermute(f_next, axis_key, [(s, s ^ k0) for s in range(met_up)])  47.8 us
    all_gather x1, waiting for transfers between devices, body(): gathered = lax.all_gather(panel_factor, 'col', axis=1, tiled=True)  32.4 us
    ppermute x15, starting transfers between devices, _choose_record(): lax.ppermute(f_next, axis_key, [(s, s ^ k0) for s in range(met_up)])  20.6 us
    another operation x3, other arithmetic, body(): lower_factor = jnp.linalg.cholesky(shared[:panel_width])  6.52 us
    dot_general x1, matrix products, body(): lax.dot_general(gathered, slab_factor, (((0,), (0,)), ((), ())), precisio...  6 us
  transfers between devices with their start and end apart: 18, of which 12 were waited for; matrix products, arithmetic and copies ran while one was open for 0% of the time, Pallas kernels for 0%

profile of v1, /device:TPU:0, one launch (start us, length us, event | category | flops | bytes accessed | tf_op | source)
XLA Modules:
  0.0 288.6 jit_solution(18054009681356506962)
XLA Ops:
  7.2 0.0 all-reduce.3.cloned.1.call-start
  7.2 0.8 slice.34
  8.0 0.1 copy.22
  8.1 1.1 copy.17
  9.2 0.7 maximum_select_fusion
  9.9 0.0 all-reduce.3.cloned.1.call-update
  9.9 0.0 all-reduce.5.cloned.1.call-start
  10.1 143.2 %all-reduce.3.cloned.1.call-done = f32[320,64]{0,1:T(8,128)} async-done(((f32[320,64]{0,1:T(8,128)}), f32[320,64]{0,1:T(8,128)}) %all-reduce.3.cloned.1.call-update) | async-done | bytes 81936 | tf_op jit(solution)/shard_map/psum | solution.py:38
  153.3 0.8 slice.45
  154.1 0.1 copy.18
  154.1 0.8 fusion.5
  154.9 5.8 %cholesky.18 = f32[64,64]{1,0:T(8,128)S(1)} custom-call(f32[64,64]{1,0:T(8,128)S(1)} %fusion.5), custom_call_target="Cholesky" | custom-call | tf_op jit(solution)/shard_map/jit(cholesky)/cholesky | solution.py:53
  160.8 0.6 compare_reduce_fusion
  161.4 0.7 fusion.1
  162.1 4.9 %custom-call.7 = f32[1,64,64]{1,2,0:T(8,128)S(1)} custom-call(f32[1,64,64]{2,1,0:T(8,128)S(1)} %fusion.1), custom_call_target="InvertDiagBlocksLowerTriangular" | custom-call | tf_op jit(solution)/shard_map/jit(_solve_triangular)/triangular_solve | solution.py:42
  167.0 1.7 broadcast_select_fusion
  168.7 0.0 copy-start
  168.7 1.2 fusion
  169.9 0.4 convolution_subtract_fusion.1
  170.4 0.1 copy.20
  170.6 0.0 all-reduce.5.cloned.1.call-update
  170.6 0.0 all-gather.2.cloned.1.call-start
  170.7 0.1 dynamic-slice_bitcast_fusion
  170.7 2.4 collective-permute-start
  173.1 0.0 copy-done
  173.2 0.0 all-gather.2.cloned.1.call-update
  173.2 2.1 collective-permute-start.14
  175.3 2.6 collective-permute-start.13
  177.9 1.5 collective-permute-start.12
  179.4 2.7 collective-permute-start.11
  182.1 0.0 collective-permute-done
  182.1 1.8 collective-permute-start.1
  184.0 3.4 %collective-permute-done.1 = f32[16,256]{1,0:T(8,128)S(1)} collective-permute-done((f32[16,256]{1,0:T(8,128)S(1)}, f32[16,256]{1,0:T(8,128)S(1)}, u32[]{:S(2)}, u32[]{:S(2)}) %collective-permute-start.1) | collective-permute-done | bytes 16416 | tf_op jit(solution)/shard_map/ppermute | solution.py:29
  187.4 1.9 collective-permute-start.2
  189.3 3.0 %collective-permute-done.2 = f32[16,256]{1,0:T(8,128)S(1)} collective-permute-done((f32[16,256]{1,0:T(8,128)S(1)}, f32[16,256]{1,0:T(8,128)S(1)}, u32[]{:S(2)}, u32[]{:S(2)}) %collective-permute-start.2) | collective-permute-done | bytes 16416 | tf_op jit(solution)/shard_map/ppermute | solution.py:29
  192.3 0.0 collective-permute-start.3
  192.3 3.7 %collective-permute-done.3 = f32[16,256]{1,0:T(8,128)S(1)} collective-permute-done((f32[16,256]{1,0:T(8,128)S(1)}, f32[16,256]{1,0:T(8,128)S(1)}, u32[]{:S(2)}, u32[]{:S(2)}) %collective-permute-start.3) | collective-permute-done | bytes 16416 | tf_op jit(solution)/shard_map/ppermute | solution.py:29
  196.1 0.0 collective-permute-start.4
  196.1 4.6 %collective-permute-done.4 = f32[16,256]{1,0:T(8,128)S(1)} collective-permute-done((f32[16,256]{1,0:T(8,128)S(1)}, f32[16,256]{1,0:T(8,128)S(1)}, u32[]{:S(2)}, u32[]{:S(2)}) %collective-permute-start.4) | collective-permute-done | bytes 16416 | tf_op jit(solution)/shard_map/ppermute | solution.py:29
  200.7 1.3 collective-permute-start.5
  202.1 4.8 %collective-permute-done.5 = f32[16,256]{1,0:T(8,128)S(1)} collective-permute-done((f32[16,256]{1,0:T(8,128)S(1)}, f32[16,256]{1,0:T(8,128)S(1)}, u32[]{:S(2)}, u32[]{:S(2)}) %collective-permute-start.5) | collective-permute-done | bytes 16416 | tf_op jit(solution)/shard_map/ppermute | solution.py:29
  206.9 1.3 collective-permute-start.6
  208.2 4.5 %collective-permute-done.6 = f32[16,256]{1,0:T(8,128)S(1)} collective-permute-done((f32[16,256]{1,0:T(8,128)S(1)}, f32[16,256]{1,0:T(8,128)S(1)}, u32[]{:S(2)}, u32[]{:S(2)}) %collective-permute-start.6) | collective-permute-done | bytes 16416 | tf_op jit(solution)/shard_map/ppermute | solution.py:29
  212.7 0.0 collective-permute-start.7
  212.7 5.2 %collective-permute-done.7 = f32[16,256]{1,0:T(8,128)S(1)} collective-permute-done((f32[16,256]{1,0:T(8,128)S(1)}, f32[16,256]{1,0:T(8,128)S(1)}, u32[]{:S(2)}, u32[]{:S(2)}) %collective-permute-start.7) | collective-permute-done | bytes 16416 | tf_op jit(solution)/shard_map/ppermute | solution.py:29
  218.0 0.0 collective-permute-start.8
  218.0 6.1 %collective-permute-done.8 = f32[16,256]{1,0:T(8,128)S(1)} collective-permute-done((f32[16,256]{1,0:T(8,128)S(1)}, f32[16,256]{1,0:T(8,128)S(1)}, u32[]{:S(2)}, u32[]{:S(2)}) %collective-permute-start.8) | collective-permute-done | bytes 16416 | tf_op jit(solution)/shard_map/ppermute | solution.py:29
  224.1 1.3 collective-permute-start.9
  225.4 6.3 %collective-permute-done.9 = f32[16,256]{1,0:T(8,128)S(1)} collective-permute-done((f32[16,256]{1,0:T(8,128)S(1)}, f32[16,256]{1,0:T(8,128)S(1)}, u32[]{:S(2)}, u32[]{:S(2)}) %collective-permute-start.9) | collective-permute-done | bytes 16416 | tf_op jit(solution)/shard_map/ppermute | solution.py:29
  231.8 1.5 collective-permute-start.10
  233.2 5.9 %collective-permute-done.10 = f32[16,256]{1,0:T(8,128)S(1)} collective-permute-done((f32[16,256]{1,0:T(8,128)S(1)}, f32[16,256]{1,0:T(8,128)S(1)}, u32[]{:S(2)}, u32[]{:S(2)}) %collective-permute-start.10) | collective-permute-done | bytes 16416 | tf_op jit(solution)/shard_map/ppermute | solution.py:29
  239.1 0.0 collective-permute-done.11
  239.1 0.0 collective-permute-done.12
  239.2 0.0 collective-permute-done.13
  239.2 0.0 collective-permute-done.14
  239.2 0.6 gather_fusion
  239.8 0.7 copy.23
  240.5 0.0 all-reduce.5.cloned.1.call-done
  240.5 32.4 %all-gather.2.cloned.1.call-done = f32[64,4096]{1,0:T(8,128)} async-done(((f32[64,256]{1,0:T(8,128)}), f32[64,4096]{1,0:T(8,128)}) %all-gather.2.cloned.1.call-update) | async-done | bytes 1048592 | tf_op jit(solution)/shard_map/all_gather | solution.py:55
  272.9 6.0 %convolution_subtract_fusion = f32[4096,256]{1,0:T(8,128)S(1)} fusion(f32[4096,256]{1,0:T(8,128)} %param.6, f32[64,4096]{1,0:T(8,128)} %all-gather.2.cloned.1.call-done, f32[64,256]{1,0:T(8,128)} %all-reduce.5.cloned.1.call-done), kind=kOutput, calls=%fused_computation.1 | convolution fusion | flops 806354944 | bytes 9502720 | tf_op jit(solution)/shard_map/dot_general | solution.py:57
  278.9 0.0 copy-start.1
  278.9 0.3 slice.47
  279.2 0.6 copy-done.1
  279.7 2.3 pad_maximum_fusion
  (23 shorter events, 0.1 us)
Async XLA Ops:
  7.2 146.1 %all-reduce.3.cloned.1.call-start = ((), (), s32[]{:S(2)}) async-start(), calls=%async_computation | async-start | bytes 196608 | tf_op jit(solution)/shard_map/psum | solution.py:38
  9.9 230.6 %all-reduce.5.cloned.1.call-start = ((), (), s32[]{:S(2)}) async-start(), calls=%async_computation.1 | async-start | bytes 131072 | tf_op jit(solution)/shard_map/psum | solution.py:38
  168.7 4.4 %copy-start = (f32[64,256]{1,0:T(8,128)}, f32[64,256]{1,0:T(8,128)S(1)}, u32[]{:S(2)}) copy-start(f32[64,256]{1,0:T(8,128)S(1)} %get-tuple-element.21) | copy-start | bytes 196612
  170.6 102.3 %all-gather.2.cloned.1.call-start = ((), (), s32[]{:S(2)}) async-start(), calls=%async_computation.2 | async-start | bytes 1114112 | tf_op jit(solution)/shard_map/all_gather | solution.py:55
  170.7 11.4 %collective-permute-start = (f32[16,256]{1,0:T(8,128)S(1)}, f32[16,256]{1,0:T(8,128)S(1)}, u32[]{:S(2)}, u32[]{:S(2)}) collective-permute-start(f32[16,256]{1,0:T(8,128)S(1)} %get-tuple-element.18), channel_id=1, source_target_pairs={{0,1},{1,0},{2,3},{3,2},{4,5},{5,4},{6,7},{7,6},{8,9},{9,8},{10,11... | collective-permute-start | bytes 49160 | tf_op jit(solution)/shard_map/ppermute | solution.py:29
  173.2 66.0 %collective-permute-start.14 = (f32[16,256]{1,0:T(8,128)S(1)}, f32[16,256]{1,0:T(8,128)S(1)}, u32[]{:S(2)}, u32[]{:S(2)}) collective-permute-start(f32[16,256]{1,0:T(8,128)S(1)} %get-tuple-element.4), channel_id=1, source_target_pairs={{0,15},{1,14},{2,13},{3,12},{4,11},{5,10},{6,9},{7,8},{8,7},{9,6},... | collective-permute-start | bytes 49160 | tf_op jit(solution)/shard_map/ppermute | solution.py:29
  175.3 63.8 %collective-permute-start.13 = (f32[16,256]{1,0:T(8,128)S(1)}, f32[16,256]{1,0:T(8,128)S(1)}, u32[]{:S(2)}, u32[]{:S(2)}) collective-permute-start(f32[16,256]{1,0:T(8,128)S(1)} %get-tuple-element.5), channel_id=1, source_target_pairs={{0,14},{1,15},{2,12},{3,13},{4,10},{5,11},{6,8},{7,9},{8,6},{9,7},... | collective-permute-start | bytes 49160 | tf_op jit(solution)/shard_map/ppermute | solution.py:29
  177.9 61.2 %collective-permute-start.12 = (f32[16,256]{1,0:T(8,128)S(1)}, f32[16,256]{1,0:T(8,128)S(1)}, u32[]{:S(2)}, u32[]{:S(2)}) collective-permute-start(f32[16,256]{1,0:T(8,128)S(1)} %get-tuple-element.6), channel_id=1, source_target_pairs={{0,13},{1,12},{2,15},{3,14},{4,9},{5,8},{6,11},{7,10},{8,5},{9,4},... | collective-permute-start | bytes 49160 | tf_op jit(solution)/shard_map/ppermute | solution.py:29
  179.4 59.7 %collective-permute-start.11 = (f32[16,256]{1,0:T(8,128)S(1)}, f32[16,256]{1,0:T(8,128)S(1)}, u32[]{:S(2)}, u32[]{:S(2)}) collective-permute-start(f32[16,256]{1,0:T(8,128)S(1)} %get-tuple-element.7), channel_id=1, source_target_pairs={{0,12},{1,13},{2,14},{3,15},{4,8},{5,9},{6,10},{7,11},{8,4},{9,5},... | collective-permute-start | bytes 49160 | tf_op jit(solution)/shard_map/ppermute | solution.py:29
  182.1 5.2 %collective-permute-start.1 = (f32[16,256]{1,0:T(8,128)S(1)}, f32[16,256]{1,0:T(8,128)S(1)}, u32[]{:S(2)}, u32[]{:S(2)}) collective-permute-start(f32[16,256]{1,0:T(8,128)S(1)} %get-tuple-element.17), channel_id=1, source_target_pairs={{0,2},{1,3},{2,0},{3,1},{4,6},{5,7},{6,4},{7,5},{8,10},{9,11},{10,... | collective-permute-start | bytes 49160 | tf_op jit(solution)/shard_map/ppermute | solution.py:29
  187.4 4.9 %collective-permute-start.2 = (f32[16,256]{1,0:T(8,128)S(1)}, f32[16,256]{1,0:T(8,128)S(1)}, u32[]{:S(2)}, u32[]{:S(2)}) collective-permute-start(f32[16,256]{1,0:T(8,128)S(1)} %get-tuple-element.16), channel_id=1, source_target_pairs={{0,3},{1,2},{2,1},{3,0},{4,7},{5,6},{6,5},{7,4},{8,11},{9,10},{10,... | collective-permute-start | bytes 49160 | tf_op jit(solution)/shard_map/ppermute | solution.py:29
  192.3 3.7 %collective-permute-start.3 = (f32[16,256]{1,0:T(8,128)S(1)}, f32[16,256]{1,0:T(8,128)S(1)}, u32[]{:S(2)}, u32[]{:S(2)}) collective-permute-start(f32[16,256]{1,0:T(8,128)S(1)} %get-tuple-element.15), channel_id=1, source_target_pairs={{0,4},{1,5},{2,6},{3,7},{4,0},{5,1},{6,2},{7,3},{8,12},{9,13},{10,... | collective-permute-start | bytes 49160 | tf_op jit(solution)/shard_map/ppermute | solution.py:29
  196.1 4.6 %collective-permute-start.4 = (f32[16,256]{1,0:T(8,128)S(1)}, f32[16,256]{1,0:T(8,128)S(1)}, u32[]{:S(2)}, u32[]{:S(2)}) collective-permute-start(f32[16,256]{1,0:T(8,128)S(1)} %get-tuple-element.14), channel_id=1, source_target_pairs={{0,5},{1,4},{2,7},{3,6},{4,1},{5,0},{6,3},{7,2},{8,13},{9,12},{10,... | collective-permute-start | bytes 49160 | tf_op jit(solution)/shard_map/ppermute | solution.py:29
  200.7 6.1 %collective-permute-start.5 = (f32[16,256]{1,0:T(8,128)S(1)}, f32[16,256]{1,0:T(8,128)S(1)}, u32[]{:S(2)}, u32[]{:S(2)}) collective-permute-start(f32[16,256]{1,0:T(8,128)S(1)} %get-tuple-element.13), channel_id=1, source_target_pairs={{0,6},{1,7},{2,4},{3,5},{4,2},{5,3},{6,0},{7,1},{8,14},{9,15},{10,... | collective-permute-start | bytes 49160 | tf_op jit(solution)/shard_map/ppermute | solution.py:29
  206.9 5.9 %collective-permute-start.6 = (f32[16,256]{1,0:T(8,128)S(1)}, f32[16,256]{1,0:T(8,128)S(1)}, u32[]{:S(2)}, u32[]{:S(2)}) collective-permute-start(f32[16,256]{1,0:T(8,128)S(1)} %get-tuple-element.12), channel_id=1, source_target_pairs={{0,7},{1,6},{2,5},{3,4},{4,3},{5,2},{6,1},{7,0},{8,15},{9,14},{10,... | collective-permute-start | bytes 49160 | tf_op jit(solution)/shard_map/ppermute | solution.py:29
  212.7 5.2 %collective-permute-start.7 = (f32[16,256]{1,0:T(8,128)S(1)}, f32[16,256]{1,0:T(8,128)S(1)}, u32[]{:S(2)}, u32[]{:S(2)}) collective-permute-start(f32[16,256]{1,0:T(8,128)S(1)} %get-tuple-element.11), channel_id=1, source_target_pairs={{0,8},{1,9},{2,10},{3,11},{4,12},{5,13},{6,14},{7,15},{8,0},{9,1},... | collective-permute-start | bytes 49160 | tf_op jit(solution)/shard_map/ppermute | solution.py:29
  218.0 6.1 %collective-permute-start.8 = (f32[16,256]{1,0:T(8,128)S(1)}, f32[16,256]{1,0:T(8,128)S(1)}, u32[]{:S(2)}, u32[]{:S(2)}) collective-permute-start(f32[16,256]{1,0:T(8,128)S(1)} %get-tuple-element.10), channel_id=1, source_target_pairs={{0,9},{1,8},{2,11},{3,10},{4,13},{5,12},{6,15},{7,14},{8,1},{9,0},... | collective-permute-start | bytes 49160 | tf_op jit(solution)/shard_map/ppermute | solution.py:29
  224.1 7.6 %collective-permute-start.9 = (f32[16,256]{1,0:T(8,128)S(1)}, f32[16,256]{1,0:T(8,128)S(1)}, u32[]{:S(2)}, u32[]{:S(2)}) collective-permute-start(f32[16,256]{1,0:T(8,128)S(1)} %get-tuple-element.9), channel_id=1, source_target_pairs={{0,10},{1,11},{2,8},{3,9},{4,14},{5,15},{6,12},{7,13},{8,2},{9,3},... | collective-permute-start | bytes 49160 | tf_op jit(solution)/shard_map/ppermute | solution.py:29
  231.8 7.4 %collective-permute-start.10 = (f32[16,256]{1,0:T(8,128)S(1)}, f32[16,256]{1,0:T(8,128)S(1)}, u32[]{:S(2)}, u32[]{:S(2)}) collective-permute-start(f32[16,256]{1,0:T(8,128)S(1)} %get-tuple-element.8), channel_id=1, source_target_pairs={{0,11},{1,10},{2,9},{3,8},{4,15},{5,14},{6,13},{7,12},{8,3},{9,2},... | collective-permute-start | bytes 49160 | tf_op jit(solution)/shard_map/ppermute | solution.py:29
  278.9 0.8 copy-start.1
Sparse Core Ops, SparseCore 0:
  13.3 139.9 all-reduce.2
  170.7 56.8 all-reduce.4
  230.3 42.5 all-gather.1
